TPU v7x, 32 devices: a whole 2x2x4 slice. The times are simulated.
32 devices in a mesh: row: 8 (over y, x, core), col: 4 (over z).
Axes of the slice: x: 2, y: 2, z: 4, core: 2. Of those that a mesh axis runs over, the one named last changes fastest.
Arguments:
- integrals: float32 [262144, 1024], P(('row', 'col')), may hold values from -0.1875 to 0.1875
- amplitudes: float32 [64, 32768], P(None, ('row', 'col')), may hold values from -6 to 6
Outputs:
- ladder: float32 [16384, 32768], P('row', 'col')
All inputs are finite; a program needn't handle non-finite values.
Results may differ from a plain program's by a relative error of at most 0.00007.
Values sent between devices are 32-bit elements; how exact they have to be, the bound alone decides.
No kernel may reach another device: no remote copies, remote signals or barrier semaphores. Data moves between devices by JAX's collectives and lax.ppermute only.
A program may use at most 448 MiB of HBM per device.

v0:
```python
import jax
import jax.numpy as jnp
from jax import lax
from jax.sharding import PartitionSpec as P

NV = 512
NO = 64
NI = 32
NC = 2


def arrange(flat_amps):
    return flat_amps.reshape(NC, NI, NV, NO).transpose(0, 2, 1, 3).reshape(NC * NV, NI * NO)


def body(integrals, amplitudes):
    flat_amps = lax.all_gather(amplitudes, ("row", "col"), axis=1, tiled=True)
    panel_amps = arrange(flat_amps)
    col_count = lax.axis_size("col")
    local_avals = integrals.shape[0] // NV
    b_width = NV // col_count
    blocks = integrals.reshape(local_avals, col_count, b_width, NC * NV)
    piece = lax.all_to_all(blocks, "col", split_axis=1, concat_axis=0, tiled=True)
    leading = piece.shape[:3]
    result = jnp.dot(
        piece.reshape(-1, NC * NV),
        panel_amps,
        precision=lax.Precision.HIGHEST,
        preferred_element_type=jnp.float32,
    )
    moved = result.reshape(leading + (NI * NO,))
    group_avals = moved.shape[0]
    ladder = moved.reshape(group_avals, b_width, NI, NO).transpose(0, 2, 1, 3)
    return ladder.reshape(group_avals * NI, b_width * NO)


def solution(mesh):
    return jax.shard_map(
        body,
        mesh=mesh,
        in_specs=(P(("row", "col"), None), P(None, ("row", "col"))),
        out_specs=P("row", "col"),
        check_vma=False,
    )
```

profile of v0, /device:TPU:25, one launch (start us, length us, event | category | flops | bytes accessed | tf_op | source)
XLA Modules:
  0.0 1263.3 jit_solution(9209612362592736215)
XLA Ops:
  6.5 23.5 %copy.7 = f32[16,4,128,1024]{3,2,0,1:T(8,128)} copy(f32[16,4,128,1024]{3,2,1,0:T(8,128)} %bitcast.30) | data formatting | bytes 67108864 | tf_op jit(solution)/shard_map/reshape | solution.py:22
  30.1 9.7 all-to-all-start
  39.8 0.0 all-gather.2.cloned.1.call-start
  39.8 0.7 all-gather.2.cloned.1.call-update
  40.5 762.1 %all-gather.2.cloned.1.call-done = f32[64,32768]{1,0:T(8,128)} async-done(((f32[64,1024]{1,0:T(8,128)}), f32[64,32768]{1,0:T(8,128)}) %all-gather.2.cloned.1.call-update) | async-done | bytes 8388624 | tf_op jit(solution)/shard_map/all_gather | solution.py:17
  802.6 13.1 %reshape.18 = f32[2,32,512,64]{3,2,1,0:T(8,128)} reshape(f32[64,32768]{1,0:T(8,128)} %all-gather.2.cloned.1.call-done) | data formatting | bytes 16777216 | tf_op jit(solution)/shard_map/reshape | solution.py:13
  815.7 15.8 %copy.8 = f32[2,512,32,64]{1,0,3,2:T(2,128)} copy(f32[2,512,32,64]{3,1,2,0:T(8,128)} %bitcast.28) | data formatting | bytes 16777216 | tf_op jit(solution)/shard_map/transpose | solution.py:13
  831.5 8.7 copy.11
  840.2 0.0 all-to-all-done
  840.2 221.4 %convolution_bitcast_fusion = f32[64,32,128,64]{2,3,1,0:T(8,128)} fusion(f32[64,128,1024,1]{2,1,3,0:T(8,128)} %bitcast.5, f32[32,64,1024,1]{2,1,0,3:T(8,128)} %bitcast.31), kind=kOutput, calls=%fused_computation | convolution fusion | flops 206158430208 | bytes 109051904 | tf_op jit(solution)/shard_map/dot_general | solution.py:25
  1061.6 87.0 %copy.9 = f32[64,32,128,64]{3,2,1,0:T(8,128)} copy(f32[64,32,128,64]{2,3,1,0:T(8,128)} %convolution_bitcast_fusion) | data formatting | bytes 134217728 | tf_op jit(solution)/shard_map/transpose | solution.py:33
  1148.6 107.9 %reshape.20 = f32[2048,8192]{1,0:T(8,128)} reshape(f32[64,32,128,64]{3,2,1,0:T(8,128)} %copy.9) | data formatting | bytes 134217728 | tf_op jit(solution)/shard_map/reshape | solution.py:34
Async XLA Ops:
  30.1 810.1 %all-to-all-start = ((f32[16,4,128,1024]{3,2,0,1:T(8,128)}), f32[16,4,128,1024]{3,2,0,1:T(8,128)}, u32[]{:S(2)}, u32[]{:S(2)}) async-start(f32[16,4,128,1024]{3,2,0,1:T(8,128)} %copy.7), calls=%async_computation | async-start | bytes 67108864 | tf_op jit(solution)/shard_map/all_to_all | solution.py:23
  39.8 762.8 %all-gather.2.cloned.1.call-start = ((), (), s32[]{:S(2)}) async-start(), calls=%async_computation.1 | async-start | bytes 8650752 | tf_op jit(solution)/shard_map/all_gather | solution.py:17
Sparse Core Ops, SparseCore 0:
  43.6 758.9 all-gather.1
where the time goes:
time: 1270 us; the launch traced here: 1260 us
  waiting for transfers between devices  763 us (60%)
  local copies, waits for them, and re-layouts  256 us (20%)
  matrix products  221 us (17%)
  between operations  13.4 us (1%)
    all_gather x1, waiting for transfers between devices, body(): flat_amps = lax.all_gather(amplitudes, ('row', 'col'), axis=1, tiled=True)  762 us
    dot_general x1, matrix products, body(): jnp.dot(piece.reshape(-1, NC * NV), panel_amps, precision=lax.Precision.H...  221 us
    reshape x1, local copies, waits for them, and re-layouts, body(): return ladder.reshape(group_avals * NI, b_width * NO)  108 us
    transpose x1, local copies, waits for them, and re-layouts, body(): ladder = moved.reshape(group_avals, b_width, NI, NO).transpose(0, 2, 1, 3)  87 us
  transfers between devices with their start and end apart: 2, of which 1 were waited for; matrix products, arithmetic and copies ran while one was open for 3% of the time, Pallas kernels for 0%

commit v1 on v0

--- a/solution.py
+++ b/solution.py
@@ -14,7 +14,15 @@
 
 
 def body(integrals, amplitudes):
-    flat_amps = lax.all_gather(amplitudes, ("row", "col"), axis=1, tiled=True)
+    ways, here = (lax.axis_size(("row", "col")), lax.axis_index(("row", "col")))
+    grown, reach = (amplitudes, 1)
+    while reach < ways:
+        theirs = lax.ppermute(grown, ("row", "col"), [(d, d ^ reach) for d in range(ways)])
+        mine_first = jnp.concatenate([grown, theirs], axis=1)
+        theirs_first = jnp.concatenate([theirs, grown], axis=1)
+        grown = jnp.where(here & reach == 0, mine_first, theirs_first)
+        reach = 2 * reach
+    flat_amps = grown
     panel_amps = arrange(flat_amps)
     col_count = lax.axis_size("col")
     local_avals = integrals.shape[0] // NV

time: 1270 us -> 1460 us (1.15)
  waiting for transfers between devices: 763 us -> 879 us
  local copies, waits for them, and re-layouts: 256 us -> 301 us
  matrix products: 221 us -> 237 us
  other arithmetic: 0 us -> 15.9 us
    ppermute x0 -> x5, waiting for transfers between devices: none -> 879 us  [body(): lax.ppermute(grown, ('row', 'col'), [(d, d ^ reach) for d in range(ways)])]
    all_gather x1 -> x0, waiting for transfers between devices: 762 us -> none  [body(): flat_amps = lax.all_gather(amplitudes, ('row', 'col'), axis=1, tiled=True)]
    another operation x0 -> x1, local copies, waits for them, and re-layouts: none -> 88 us  [body(): ladder = moved.reshape(group_avals, b_width, NI, NO).transpose(0, 2, 1, 3)]
    transpose x1 -> x0, local copies, waits for them, and re-layouts: 87 us -> none  [body(): ladder = moved.reshape(group_avals, b_width, NI, NO).transpose(0, 2, 1, 3)]
    unnamed x1 -> x4, local copies, waits for them, and re-layouts: 8.67 us -> 53 us
    select_n x0 -> x5, other arithmetic: none -> 15.9 us  [body(): grown = jnp.where(here & reach == 0, mine_first, theirs_first)]
    dot_general x1, matrix products: 221 us -> 237 us  [body(): jnp.dot(piece.reshape(-1, NC * NV), panel_amps, precision=lax.Precision.H...]
  transfers between devices with their start and end apart: 2 -> 6, of which waited for: 1 -> 5; matrix products, arithmetic and copies ran while one was open for 3% -> 4% of each run, Pallas kernels for 0% -> 0%
where the time goes in v1:
time: 1460 us; the launch traced here: 1450 us
  waiting for transfers between devices  879 us (60%)
  local copies, waits for them, and re-layouts  301 us (21%)
  matrix products  237 us (16%)
  other arithmetic  15.9 us (1%)
  starting transfers between devices  15.1 us (1%)
    ppermute x5, waiting for transfers between devices, body(): lax.ppermute(grown, ('row', 'col'), [(d, d ^ reach) for d in range(ways)])  879 us
    dot_general x1, matrix products, body(): jnp.dot(piece.reshape(-1, NC * NV), panel_amps, precision=lax.Precision.H...  237 us
    reshape x1, local copies, waits for them, and re-layouts, body(): return ladder.reshape(group_avals * NI, b_width * NO)  108 us
    another operation x1, local copies, waits for them, and re-layouts, body(): ladder = moved.reshape(group_avals, b_width, NI, NO).transpose(0, 2, 1, 3)  88 us
    unnamed x4, local copies, waits for them, and re-layouts  53 us
  transfers between devices with their start and end apart: 6, of which 5 were waited for; matrix products, arithmetic and copies ran while one was open for 4% of the time, Pallas kernels for 0%

profile of v1, /device:TPU:25, one launch (start us, length us, event | category | flops | bytes accessed | tf_op | source)
XLA Modules:
  0.0 1448.3 jit_solution(17161594041527176394)
XLA Ops:
  0.0 23.5 %copy.10 = f32[16,4,128,1024]{3,2,0,1:T(8,128)} copy(f32[16,4,128,1024]{3,2,1,0:T(8,128)} %bitcast.26) | data formatting | bytes 67108864 | tf_op jit(solution)/shard_map/reshape | solution.py:30
  23.5 0.0 copy-start
  23.5 9.8 all-to-all-start
  33.4 0.0 copy-done
  33.4 0.2 collective-permute-start
  33.6 544.6 %collective-permute-done = f32[64,1024]{1,0:T(8,128)S(1)} collective-permute-done((f32[64,1024]{1,0:T(8,128)S(1)}, f32[64,1024]{1,0:T(8,128)S(1)}, u32[]{:S(2)}, u32[]{:S(2)}) %collective-permute-start) | collective-permute-done | bytes 262176 | tf_op jit(solution)/shard_map/ppermute | solution.py:20
  578.3 0.8 collective-permute-start.1
  579.1 196.4 %collective-permute-done.1 = f32[64,2048]{1,0:T(8,128)S(1)} collective-permute-done((f32[64,2048]{1,0:T(8,128)S(1)}, f32[64,2048]{1,0:T(8,128)S(1)}, u32[]{:S(2)}, u32[]{:S(2)}) %collective-permute-start.1) | collective-permute-done | bytes 524320 | tf_op jit(solution)/shard_map/ppermute | solution.py:20
  775.5 0.1 maximum_select_fusion.3
  775.7 1.3 collective-permute-start.2
  777.0 2.4 collective-permute-done.2
  779.4 1.8 maximum_select_fusion.2
  781.2 1.5 collective-permute-start.3
  782.6 45.5 %collective-permute-done.3 = f32[64,8192]{1,0:T(8,128)} collective-permute-done((f32[64,8192]{1,0:T(8,128)S(1)}, f32[64,8192]{1,0:T(8,128)}, u32[]{:S(2)}, u32[]{:S(2)}) %collective-permute-start.3) | collective-permute-done | bytes 2097184 | tf_op jit(solution)/shard_map/ppermute | solution.py:20
  828.2 4.7 maximum_select_fusion.1
  832.9 1.4 collective-permute-start.4
  834.3 89.8 %collective-permute-done.4 = f32[64,16384]{1,0:T(8,128)} collective-permute-done((f32[64,16384]{1,0:T(8,128)}, f32[64,16384]{1,0:T(8,128)}, u32[]{:S(2)}, u32[]{:S(2)}) %collective-permute-start.4) | collective-permute-done | bytes 4194336 | tf_op jit(solution)/shard_map/ppermute | solution.py:20
  924.1 9.2 maximum_select_fusion
  933.3 13.1 select_n.54
  946.5 15.8 %copy.9 = f32[2,512,32,64]{1,0,3,2:T(2,128)} copy(f32[2,512,32,64]{3,1,2,0:T(8,128)} %bitcast.24) | data formatting | bytes 16777216 | tf_op jit(solution)/shard_map/transpose | solution.py:13
  962.3 8.7 copy.12
  970.9 0.0 all-to-all-done
  970.9 237.1 %convolution_bitcast_fusion = f32[256,8,64,128]{3,1,2,0:T(8,128)} fusion(f32[1024,2048]{0,1:T(8,128)} %bitcast.27, f32[8192,1024]{1,0:T(8,128)} %bitcast.4), kind=kOutput, calls=%fused_computation | convolution fusion | flops 206158430208 | bytes 109051904 | tf_op jit(solution)/shard_map/dot_general | solution.py:33
  1208.1 44.3 %copy.13 = f32[256,8,64,128]{3,2,1,0:T(8,128)} copy(f32[256,8,64,128]{3,1,2,0:T(8,128)} %convolution_bitcast_fusion) | data formatting | bytes 134217728
  1252.3 88.0 %copy.11 = f32[64,128,32,64]{3,1,2,0:T(8,128)} copy(f32[64,128,32,64]{1,0,3,2:T(8,128)} %bitcast.18) | data formatting | bytes 134217728 | tf_op jit(solution)/shard_map/reshape;reshape | solution.py:41
  1340.4 107.9 %reshape.21 = f32[2048,8192]{1,0:T(8,128)} reshape(f32[64,32,128,64]{3,2,1,0:T(8,128)} %bitcast.6) | data formatting | bytes 134217728 | tf_op jit(solution)/shard_map/reshape | solution.py:42
  (1 shorter events, 0.0 us)
Async XLA Ops:
  23.5 9.9 copy-start
  23.5 947.4 %all-to-all-start = ((f32[16,4,128,1024]{3,2,0,1:T(8,128)}), f32[16,4,128,1024]{3,2,0,1:T(8,128)}, u32[]{:S(2)}, u32[]{:S(2)}) async-start(f32[16,4,128,1024]{3,2,0,1:T(8,128)} %copy.10), calls=%async_computation | async-start | bytes 67108864 | tf_op jit(solution)/shard_map/all_to_all | solution.py:31
  33.4 544.8 %collective-permute-start = (f32[64,1024]{1,0:T(8,128)S(1)}, f32[64,1024]{1,0:T(8,128)S(1)}, u32[]{:S(2)}, u32[]{:S(2)}) collective-permute-start(f32[64,1024]{1,0:T(8,128)S(1)} %copy-done), channel_id=1, source_target_pairs={{0,1},{1,0},{2,3},{3,2},{4,5},{5,4},{6,7},{7,6},{8,9},{9,8},{10,11... | collective-permute-start | bytes 786440 | tf_op jit(solution)/shard_map/ppermute | solution.py:20
  578.3 197.3 %collective-permute-start.1 = (f32[64,2048]{1,0:T(8,128)S(1)}, f32[64,2048]{1,0:T(8,128)S(1)}, u32[]{:S(2)}, u32[]{:S(2)}) collective-permute-start(f32[64,2048]{1,0:T(8,128)S(1)} %maximum_select_fusion.4), channel_id=1, source_target_pairs={{0,2},{1,3},{2,0},{3,1},{4,6},{5,7},{6,4},{7,5},{8,10},{9,11},{10,... | collective-permute-start | bytes 1572872 | tf_op jit(solution)/shard_map/ppermute | solution.py:20
  775.7 3.7 collective-permute-start.2
  781.2 47.0 %collective-permute-start.3 = (f32[64,8192]{1,0:T(8,128)S(1)}, f32[64,8192]{1,0:T(8,128)}, u32[]{:S(2)}, u32[]{:S(2)}) collective-permute-start(f32[64,8192]{1,0:T(8,128)S(1)} %maximum_select_fusion.2), channel_id=1, source_target_pairs={{0,8},{1,9},{2,10},{3,11},{4,12},{5,13},{6,14},{7,15},{8,0},{9,1},... | collective-permute-start | bytes 6291464 | tf_op jit(solution)/shard_map/ppermute | solution.py:20
  832.9 91.2 %collective-permute-start.4 = (f32[64,16384]{1,0:T(8,128)}, f32[64,16384]{1,0:T(8,128)}, u32[]{:S(2)}, u32[]{:S(2)}) collective-permute-start(f32[64,16384]{1,0:T(8,128)} %maximum_select_fusion.1), channel_id=1, source_target_pairs={{0,16},{1,17},{2,18},{3,19},{4,20},{5,21},{6,22},{7,23},{8,24},{9,... | collective-permute-start | bytes 12582920 | tf_op jit(solution)/shard_map/ppermute | solution.py:20
